TPU v7x, 32 devices: a whole 2x2x4 slice. The times are simulated.
32 devices in a mesh: pool: 8 (over z, core), band: 4 (over y, x).
Axes of the slice: x: 2, y: 2, z: 4, core: 2. Of those that a mesh axis runs over, the one named last changes fastest.
Arguments:
- orbitals: float32 [8, 4, 2, 13824], P('pool', 'band'), may hold values from -6 to 6
- kpoints: float32 [8, 3], replicated, may hold values from -0.5 to 0.5
- owner: int32 [1], replicated, may hold values from 0 to 7
Outputs:
- exchange: float32 [8, 4, 2, 13824], P('pool', 'band')
All inputs are finite; a program needn't handle non-finite values.
Results may differ from a plain program's by a relative error of at most 0.0001.
Values sent between devices are 32-bit elements; how exact they have to be, the bound alone decides.
A program may use at most 64 MiB of HBM per device.

v0:
```python
import math
import jax
import jax.numpy as jnp
from jax import lax
from jax.sharding import PartitionSpec as P

NG = 24
mixing = 0.25
kernel_scale = 60.0
screening = 4.0


def frequencies():
    idx = jnp.arange(NG, dtype=jnp.int32)
    return ((idx + NG // 2) % NG - NG // 2).astype(jnp.float32)


def coulomb(dvec):
    freq = frequencies()
    square = (
        (freq[:, None, None] + dvec[0]) ** 2
        + (freq[None, :, None] + dvec[1]) ** 2
        + (freq[None, None, :] + dvec[2]) ** 2
    )
    return (kernel_scale / (square + screening)).reshape(-1)


def dft_matrix(direction, factor):
    idx = jnp.arange(NG, dtype=jnp.int32)
    phase = (idx[:, None] * idx[None, :] % NG).astype(jnp.float32) * (2.0 * math.pi / NG)
    cosine = jnp.cos(phase) * factor
    sine = direction * jnp.sin(phase) * factor
    upper = jnp.concatenate([cosine, -sine], axis=1)
    lower = jnp.concatenate([sine, cosine], axis=1)
    return jnp.concatenate([upper, lower], axis=0)


def transform(field, matrix):
    batch = field.shape[0]
    work = field.reshape(batch, 2 * NG, NG * NG)
    for turn in range(3):
        work = jnp.einsum("ij,pjk->pik", matrix, work, precision=lax.Precision.HIGHEST)
        work = (
            work.reshape(batch, 2, NG, NG, NG)
            .transpose(0, 1, 3, 4, 2)
            .reshape(batch, 2 * NG, NG * NG)
        )
    return work.reshape(batch, 2, NG * NG * NG)


def contribution(sources, resident, kernel, forward, inverse):
    count_s = sources.shape[0]
    count_r = resident.shape[0]
    src_re = sources[:, 0][:, None, :]
    src_im = sources[:, 1][:, None, :]
    res_re = resident[:, 0][None, :, :]
    res_im = resident[:, 1][None, :, :]
    dens_re = src_re * res_re + src_im * res_im
    dens_im = src_re * res_im - src_im * res_re
    density = jnp.stack([dens_re, dens_im], axis=2).reshape(count_s * count_r, 2, -1)
    spectrum = transform(density, forward) * kernel
    potential = transform(spectrum, inverse).reshape(count_s, count_r, 2, -1)
    pot_re = potential[:, :, 0]
    pot_im = potential[:, :, 1]
    out_re = -mixing * jnp.sum(src_re * pot_re - src_im * pot_im, axis=0)
    out_im = -mixing * jnp.sum(src_re * pot_im + src_im * pot_re, axis=0)
    return jnp.stack([out_re, out_im], axis=1)


def shards(orbitals, kpoints, owner):
    resident = orbitals[0]
    pool_index = lax.axis_index("pool")
    kvec = lax.dynamic_index_in_dim(kpoints, pool_index, 0, keepdims=False)
    forward = dft_matrix(-1.0, 1.0)
    inverse = dft_matrix(1.0, 1.0 / NG)
    source_k = owner[0]
    qvec = lax.dynamic_index_in_dim(kpoints, source_k, 0, keepdims=False)
    kernel = coulomb(kvec - qvec)
    masked = jnp.where(pool_index == source_k, resident, jnp.zeros_like(resident))
    sources = lax.psum(masked, "pool")
    total = contribution(
        lax.all_gather(sources, "band", axis=0, tiled=True), resident, kernel, forward, inverse
    )
    return total[None]


def solution(mesh):
    placed = (P("pool", "band", None, None), P(), P())
    return jax.shard_map(
        shards, mesh=mesh, in_specs=placed, out_specs=P("pool", "band", None, None), check_vma=False
    )
```

profile of v0, /device:TPU:8, one launch (start us, length us, event | category | flops | bytes accessed | tf_op | source)
XLA Modules:
  0.0 122.1 jit_solution(5851988328339792703)
XLA Ops:
  7.2 1.6 %broadcast_select_fusion = f32[1,2,13824]{2,1,0:T(2,128)} fusion(pred[]{:T(512)S(6)} %eq.8, f32[1,1,2,13824]{3,2,1,0:T(2,128)} %param.3), kind=kLoop, calls=%fused_computation.16 | loop fusion | flops 27648 | bytes 221185 | tf_op jit(solution)/shard_map/jit(_where)/select_n | solution.py:79
  9.0 1.3 %slice_reduce_fusion.1 = (f32[13824]{0:T(1024)S(1)}, f32[13824]{0:T(1024)S(1)}) fusion(f32[1,2,13824]{2,1,0:T(2,128)} %bitcast.81), kind=kLoop, calls=%fused_computation.19 | loop fusion | bytes 221184 | tf_op jit(solution)/shard_map/slice | solution.py:56
  12.5 1.3 %add_multiply_fusion = (f32[24]{0:T(128)S(1)}, f32[24]{0:T(128)S(1)}) fusion(f32[]{:T(128)} %bitcast.13, f32[]{:T(128)} %bitcast.12), kind=kLoop, calls=%fused_computation.43 | loop fusion | flops 312 | bytes 200 | tf_op jit(solution)/shard_map/integer_pow | solution.py:23
  14.3 50.5 %all-reduce.2.cloned.1.call-done = f32[1,2,13824]{2,1,0:T(2,128)} async-done(((f32[1,2,13824]{2,1,0:T(2,128)}), f32[1,2,13824]{2,1,0:T(2,128)}) %all-reduce.2.cloned.1.call-update) | async-done | bytes 110608 | tf_op jit(solution)/shard_map/psum | solution.py:80
  64.8 10.7 %all_gather.3 = f32[4,2,13824]{2,1,0:T(2,128)S(1)} all-gather(f32[1,2,13824]{2,1,0:T(2,128)} %all-reduce.2.cloned.1.call-done), channel_id=1, replica_groups=mesh['pool'=8,'band'=4] {'band'}, dimensions={0}, use_global_device_ids=true | all-gather | bytes 552960 | tf_op jit(solution)/shard_map/all_gather | solution.py:82
  75.9 1.4 %maximum_reduce_fusion = f32[4,2,13824]{2,1,0:T(2,128)S(1)} fusion(f32[4,1,1,13824]{3,1,2,0:T(1,128)S(1)} %get-tuple-element.10, f32[4,1,1,13824]{3,1,2,0:T(1,128)S(1)} %get-tuple-element.9), kind=kLoop, calls=%fused_computation.7 | loop fusion | flops 110592 | bytes 884736 | tf_op jit(solution)/shard_map/stack | solution.py:60
  78.3 0.9 reshape.181
  79.2 2.2 %copy.10 = f32[4,2,24,24,24]{4,3,2,1,0:T(8,128)} copy(f32[4,2,24,24,24]{3,2,4,1,0:T(8,128)S(1)} %bitcast.74) | data formatting | bytes 884736 | tf_op jit(solution)/shard_map/transpose | solution.py:45
  81.4 2.2 %reshape.182 = f32[4,48,576]{2,1,0:T(8,128)S(1)} reshape(f32[4,2,24,24,24]{4,3,2,1,0:T(8,128)} %copy.10) | data formatting | bytes 884736 | tf_op jit(solution)/shard_map/reshape | solution.py:46
  84.2 0.9 reshape.183
  85.1 2.0 %copy.11 = f32[4,2,24,24,24]{4,3,2,1,0:T(8,128)} copy(f32[4,2,24,24,24]{3,2,4,1,0:T(8,128)S(1)} %bitcast.75) | data formatting | bytes 884736 | tf_op jit(solution)/shard_map/transpose | solution.py:45
  87.1 2.2 %reshape.184 = f32[4,48,576]{2,1,0:T(8,128)S(1)} reshape(f32[4,2,24,24,24]{4,3,2,1,0:T(8,128)} %copy.11) | data formatting | bytes 884736 | tf_op jit(solution)/shard_map/reshape | solution.py:46
  89.9 0.9 reshape.185
  90.8 2.0 %copy.12 = f32[4,2,24,24,24]{4,3,2,1,0:T(8,128)} copy(f32[4,2,24,24,24]{3,2,4,1,0:T(8,128)S(1)} %bitcast.76) | data formatting | bytes 884736 | tf_op jit(solution)/shard_map/transpose | solution.py:45
  92.8 2.2 %reshape_reshape.7 = f32[4,48,576]{2,1,0:T(8,128)S(1)} reshape(f32[4,2,24,24,24]{4,3,2,1,0:T(8,128)} %copy.12) | data formatting | bytes 884736 | tf_op jit(solution)/shard_map/reshape;reshape | solution.py:48
  95.7 0.9 reshape.186
  96.6 2.0 %copy.13 = f32[4,2,24,24,24]{4,3,2,1,0:T(8,128)} copy(f32[4,2,24,24,24]{3,2,4,1,0:T(8,128)S(1)} %bitcast.77) | data formatting | bytes 884736 | tf_op jit(solution)/shard_map/transpose | solution.py:45
  98.5 2.2 %reshape.187 = f32[4,48,576]{2,1,0:T(8,128)S(1)} reshape(f32[4,2,24,24,24]{4,3,2,1,0:T(8,128)} %copy.13) | data formatting | bytes 884736 | tf_op jit(solution)/shard_map/reshape | solution.py:46
  101.4 0.9 reshape.188
  102.3 2.0 %copy.14 = f32[4,2,24,24,24]{4,3,2,1,0:T(8,128)} copy(f32[4,2,24,24,24]{3,2,4,1,0:T(8,128)S(1)} %bitcast.78) | data formatting | bytes 884736 | tf_op jit(solution)/shard_map/transpose | solution.py:45
  104.3 2.5 %reshape.189 = f32[4,48,576]{2,1,0:T(8,128)S(1)} reshape(f32[4,2,24,24,24]{4,3,2,1,0:T(8,128)} %copy.14) | data formatting | bytes 884736 | tf_op jit(solution)/shard_map/reshape | solution.py:46
  107.4 0.9 reshape.190
  108.2 2.0 %copy.15 = f32[4,2,24,24,24]{4,3,2,1,0:T(8,128)} copy(f32[4,2,24,24,24]{3,2,4,1,0:T(8,128)S(1)} %bitcast.79) | data formatting | bytes 884736 | tf_op jit(solution)/shard_map/transpose | solution.py:45
  110.2 3.3 %reshape_reshape_reshape.3 = f32[4,1,2,13824]{3,1,2,0:T(1,128)S(1)} reshape(f32[4,2,24,24,24]{4,3,2,1,0:T(8,128)} %copy.15) | data formatting | bytes 884736 | tf_op jit(solution)/shard_map/reshape;reshape;reshape | solution.py:62
  (30 shorter events, 9.0 us)
Async XLA Ops:
  6.5 58.3 %all-reduce.2.cloned.1.call-start = ((), (), s32[]{:S(2)}) async-start(), calls=%async_computation | async-start | bytes 221184 | tf_op jit(solution)/shard_map/psum | solution.py:80
Sparse Core Ops, SparseCore 0:
  9.7 55.0 all-reduce.1
where the time goes:
time: 123 us; the launch traced here: 122 us
  waiting for transfers between devices  50.5 us (41%)
  local copies, waits for them, and re-layouts  34.8 us (28%)
  between operations  14.3 us (12%)
  blocking collectives  10.7 us (9%)
  other arithmetic  8.27 us (7%)
  matrix products  3.56 us (3%)
    psum x1, waiting for transfers between devices, shards(): sources = lax.psum(masked, 'pool')  50.5 us
    transpose x6, local copies, waits for them, and re-layouts, transform(): work = work.reshape(batch, 2, NG, NG, NG).transpose(0, 1, 3, 4, 2).reshap...  12 us
    all_gather x1, blocking collectives, shards(): lax.all_gather(sources, 'band', axis=0, tiled=True)  10.7 us
    reshape x4, local copies, waits for them, and re-layouts, transform(): work = work.reshape(batch, 2, NG, NG, NG).transpose(0, 1, 3, 4, 2).reshap...  9.21 us
    reshape x6, local copies, waits for them, and re-layouts, transform(): work.reshape(batch, 2, NG, NG, NG).transpose(0, 1, 3, 4, 2)  5.29 us
    dot_general x6, matrix products, transform(): jnp.einsum('ij,pjk->pik', matrix, work, precision=lax.Precision.HIGHEST)  3.56 us
    another operation x1, local copies, waits for them, and re-layouts, contribution(): potential = transform(spectrum, inverse).reshape(count_s, count_r, 2, -1)  3.31 us
  transfers between devices with their start and end apart: 1, of which 1 were waited for; matrix products, arithmetic and copies ran while one was open for 4% of the time, Pallas kernels for 0%

commit v1 on v0

--- a/solution.py
+++ b/solution.py
@@ -8,6 +8,19 @@
 mixing = 0.25
 kernel_scale = 60.0
 screening = 4.0
+
+
+def gather_around(shard, axis, dim):
+    ways = lax.axis_size(axis)
+    up = [(d, (d + 1) % ways) for d in range(ways)]
+    down = [(d, (d - 1) % ways) for d in range(ways)]
+    earlier, later = ([shard], [shard])
+    for _ in range(ways // 2):
+        earlier.append(lax.ppermute(earlier[-1], axis, up))
+    for _ in range((ways - 1) // 2):
+        later.append(lax.ppermute(later[-1], axis, down))
+    line = jnp.concatenate([*earlier[::-1], *later[1:]], axis=dim)
+    return jnp.roll(line, (lax.axis_index(axis) - ways // 2) * shard.shape[dim], axis=dim)
 
 
 def frequencies():
@@ -78,9 +91,7 @@
     kernel = coulomb(kvec - qvec)
     masked = jnp.where(pool_index == source_k, resident, jnp.zeros_like(resident))
     sources = lax.psum(masked, "pool")
-    total = contribution(
-        lax.all_gather(sources, "band", axis=0, tiled=True), resident, kernel, forward, inverse
-    )
+    total = contribution(gather_around(sources, "band", 0), resident, kernel, forward, inverse)
     return total[None]
 
 

time: 123 us -> 127 us (1.033)
  blocking collectives: 10.7 us -> 0 us
  waiting for transfers between devices: 50.5 us -> 57.8 us
  starting transfers between devices: 0.01 us -> 4.45 us
  local copies, waits for them, and re-layouts: 34.8 us -> 37.2 us
    all_gather x1 -> x0, blocking collectives: 10.7 us -> none  [shards(): lax.all_gather(sources, 'band', axis=0, tiled=True)]
    ppermute x0 -> x3, waiting for transfers between devices: none -> 7.15 us  [the longest x2 6.91 us: gather_around(): earlier.append(lax.ppermute(earlier[-1], axis, up))]
    ppermute x0 -> x3, starting transfers between devices: none -> 4.45 us  [the longest x1 2.37 us: gather_around(): later.append(lax.ppermute(later[-1], axis, down))]
    unnamed x0 -> x11, local copies, waits for them, and re-layouts: none -> 2.33 us
  transfers between devices with their start and end apart: 1 -> 4, of which waited for: 1 -> 4; matrix products, arithmetic and copies ran while one was open for 4% -> 5% of each run, Pallas kernels for 0% -> 0%
where the time goes in v1:
time: 127 us; the launch traced here: 126 us
  waiting for transfers between devices  57.8 us (46%)
  local copies, waits for them, and re-layouts  37.2 us (29%)
  between operations  14.4 us (11%)
  other arithmetic  8.31 us (7%)
  starting transfers between devices  4.45 us (4%)
  matrix products  3.57 us (3%)
    psum x1, waiting for transfers between devices, shards(): sources = lax.psum(masked, 'pool')  50.6 us
    transpose x6, local copies, waits for them, and re-layouts, transform(): work = work.reshape(batch, 2, NG, NG, NG).transpose(0, 1, 3, 4, 2).reshap...  12 us
    reshape x4, local copies, waits for them, and re-layouts, transform(): work = work.reshape(batch, 2, NG, NG, NG).transpose(0, 1, 3, 4, 2).reshap...  9.21 us
    ppermute x2, waiting for transfers between devices, gather_around(): earlier.append(lax.ppermute(earlier[-1], axis, up))  6.91 us
    reshape x6, local copies, waits for them, and re-layouts, transform(): work.reshape(batch, 2, NG, NG, NG).transpose(0, 1, 3, 4, 2)  5.28 us
    dot_general x6, matrix products, transform(): jnp.einsum('ij,pjk->pik', matrix, work, precision=lax.Precision.HIGHEST)  3.57 us
    another operation x1, local copies, waits for them, and re-layouts, contribution(): potential = transform(spectrum, inverse).reshape(count_s, count_r, 2, -1)  3.39 us
  transfers between devices with their start and end apart: 4, of which 4 were waited for; matrix products, arithmetic and copies ran while one was open for 5% of the time, Pallas kernels for 0%

profile of v1, /device:TPU:8, one launch (start us, length us, event | category | flops | bytes accessed | tf_op | source)
XLA Modules:
  0.0 125.8 jit_solution(3084912093021170894)
XLA Ops:
  7.2 1.6 %broadcast_select_fusion = f32[1,2,13824]{2,1,0:T(2,128)} fusion(pred[]{:T(512)S(6)} %eq.11, f32[1,1,2,13824]{3,2,1,0:T(2,128)} %param.3), kind=kLoop, calls=%fused_computation.16 | loop fusion | flops 27648 | bytes 221185 | tf_op jit(solution)/shard_map/jit(_where)/select_n | solution.py:92
  8.9 1.3 %slice_reduce_fusion.1 = (f32[13824]{0:T(1024)S(1)}, f32[13824]{0:T(1024)S(1)}) fusion(f32[1,2,13824]{2,1,0:T(2,128)} %bitcast.81), kind=kLoop, calls=%fused_computation.19 | loop fusion | bytes 221184 | tf_op jit(solution)/shard_map/slice | solution.py:69
  12.3 1.3 %add_multiply_fusion = (f32[24]{0:T(128)S(1)}, f32[24]{0:T(128)S(1)}) fusion(f32[]{:T(128)} %bitcast.13, f32[]{:T(128)} %bitcast.12), kind=kLoop, calls=%fused_computation.53 | loop fusion | flops 312 | bytes 200 | tf_op jit(solution)/shard_map/integer_pow | solution.py:36
  14.2 50.6 %all-reduce.2.cloned.1.call-done = f32[1,2,13824]{2,1,0:T(2,128)} async-done(((f32[1,2,13824]{2,1,0:T(2,128)}), f32[1,2,13824]{2,1,0:T(2,128)}) %all-reduce.2.cloned.1.call-update) | async-done | bytes 110608 | tf_op jit(solution)/shard_map/psum | solution.py:93
  64.8 1.5 %collective-permute-start = (f32[1,2,13824]{2,1,0:T(2,128)}, f32[1,2,13824]{2,1,0:T(2,128)S(1)}, u32[]{:S(2)}, u32[]{:S(2)}) collective-permute-start(f32[1,2,13824]{2,1,0:T(2,128)} %all-reduce.2.cloned.1.call-done), channel_id=1, source_target_pairs={{0,1},{1,2},{2,3},{3,0},{4,5},{5,6},{6,7},{7,4},{8,9},{9,10},{10,1... | collective-permute-start | bytes 331784 | tf_op jit(solution)/shard_map/ppermute | solution.py:19
  66.3 4.3 %collective-permute-done = f32[1,2,13824]{2,1,0:T(2,128)S(1)} collective-permute-done((f32[1,2,13824]{2,1,0:T(2,128)}, f32[1,2,13824]{2,1,0:T(2,128)S(1)}, u32[]{:S(2)}, u32[]{:S(2)}) %collective-permute-start) | collective-permute-done | bytes 110624 | tf_op jit(solution)/shard_map/ppermute | solution.py:19
  71.3 2.4 %collective-permute-start.2 = (f32[1,2,13824]{2,1,0:T(2,128)}, f32[1,2,13824]{2,1,0:T(2,128)S(1)}, u32[]{:S(2)}, u32[]{:S(2)}) collective-permute-start(f32[1,2,13824]{2,1,0:T(2,128)} %all-reduce.2.cloned.1.call-done), channel_id=1, source_target_pairs={{0,3},{1,0},{2,1},{3,2},{4,7},{5,4},{6,5},{7,6},{8,11},{9,8},{10,9... | collective-permute-start | bytes 331784 | tf_op jit(solution)/shard_map/ppermute | solution.py:21
  73.7 2.6 %collective-permute-done.1 = f32[1,2,13824]{2,1,0:T(2,128)S(1)} collective-permute-done((f32[1,2,13824]{2,1,0:T(2,128)S(1)}, f32[1,2,13824]{2,1,0:T(2,128)S(1)}, u32[]{:S(2)}, u32[]{:S(2)}) %collective-permute-start.1) | collective-permute-done | bytes 110624 | tf_op jit(solution)/shard_map/ppermute | solution.py:19
  76.3 0.9 constant_dynamic-update-slice_fusion.5
  77.6 0.9 constant_dynamic-update-slice_fusion.1
  79.4 1.4 %maximum_reduce_fusion = f32[4,2,13824]{2,1,0:T(2,128)S(1)} fusion(f32[4,1,1,13824]{3,1,2,0:T(1,128)S(1)} %get-tuple-element.10, f32[4,1,1,13824]{3,1,2,0:T(1,128)S(1)} %get-tuple-element.9), kind=kLoop, calls=%fused_computation.7 | loop fusion | flops 110592 | bytes 884736 | tf_op jit(solution)/shard_map/stack | solution.py:73
  82.7 2.2 %copy.4 = f32[4,2,24,24,24]{4,3,2,1,0:T(8,128)} copy(f32[4,2,24,24,24]{3,2,4,1,0:T(8,128)S(1)} %bitcast.74) | data formatting | bytes 884736 | tf_op jit(solution)/shard_map/transpose | solution.py:58
  84.9 2.2 %reshape.182 = f32[4,48,576]{2,1,0:T(8,128)S(1)} reshape(f32[4,2,24,24,24]{4,3,2,1,0:T(8,128)} %copy.4) | data formatting | bytes 884736 | tf_op jit(solution)/shard_map/reshape | solution.py:59
  88.6 2.0 %copy.5 = f32[4,2,24,24,24]{4,3,2,1,0:T(8,128)} copy(f32[4,2,24,24,24]{3,2,4,1,0:T(8,128)S(1)} %bitcast.75) | data formatting | bytes 884736 | tf_op jit(solution)/shard_map/transpose | solution.py:58
  90.6 2.2 %reshape.184 = f32[4,48,576]{2,1,0:T(8,128)S(1)} reshape(f32[4,2,24,24,24]{4,3,2,1,0:T(8,128)} %copy.5) | data formatting | bytes 884736 | tf_op jit(solution)/shard_map/reshape | solution.py:59
  94.3 2.0 %copy.6 = f32[4,2,24,24,24]{4,3,2,1,0:T(8,128)} copy(f32[4,2,24,24,24]{3,2,4,1,0:T(8,128)S(1)} %bitcast.76) | data formatting | bytes 884736 | tf_op jit(solution)/shard_map/transpose | solution.py:58
  96.3 2.2 %reshape_reshape.7 = f32[4,48,576]{2,1,0:T(8,128)S(1)} reshape(f32[4,2,24,24,24]{4,3,2,1,0:T(8,128)} %copy.6) | data formatting | bytes 884736 | tf_op jit(solution)/shard_map/reshape;reshape | solution.py:61
  100.1 2.0 %copy.7 = f32[4,2,24,24,24]{4,3,2,1,0:T(8,128)} copy(f32[4,2,24,24,24]{3,2,4,1,0:T(8,128)S(1)} %bitcast.77) | data formatting | bytes 884736 | tf_op jit(solution)/shard_map/transpose | solution.py:58
  102.1 2.2 %reshape.187 = f32[4,48,576]{2,1,0:T(8,128)S(1)} reshape(f32[4,2,24,24,24]{4,3,2,1,0:T(8,128)} %copy.7) | data formatting | bytes 884736 | tf_op jit(solution)/shard_map/reshape | solution.py:59
  105.8 2.0 %copy.8 = f32[4,2,24,24,24]{4,3,2,1,0:T(8,128)} copy(f32[4,2,24,24,24]{3,2,4,1,0:T(8,128)S(1)} %bitcast.78) | data formatting | bytes 884736 | tf_op jit(solution)/shard_map/transpose | solution.py:58
  107.8 2.5 %reshape.189 = f32[4,48,576]{2,1,0:T(8,128)S(1)} reshape(f32[4,2,24,24,24]{4,3,2,1,0:T(8,128)} %copy.8) | data formatting | bytes 884736 | tf_op jit(solution)/shard_map/reshape | solution.py:59
  111.7 2.0 %copy.9 = f32[4,2,24,24,24]{4,3,2,1,0:T(8,128)} copy(f32[4,2,24,24,24]{3,2,4,1,0:T(8,128)S(1)} %bitcast.79) | data formatting | bytes 884736 | tf_op jit(solution)/shard_map/transpose | solution.py:58
  113.7 3.4 %reshape_reshape_reshape.3 = f32[4,1,2,13824]{3,1,2,0:T(1,128)S(1)} reshape(f32[4,2,24,24,24]{4,3,2,1,0:T(8,128)} %copy.9) | data formatting | bytes 884736 | tf_op jit(solution)/shard_map/reshape;reshape;reshape | solution.py:75
  117.1 0.9 subtract_reduce_fusion
  (47 shorter events, 14.8 us)
Async XLA Ops:
  6.5 58.3 %all-reduce.2.cloned.1.call-start = ((), (), s32[]{:S(2)}) async-start(), calls=%async_computation | async-start | bytes 221184 | tf_op jit(solution)/shard_map/psum | solution.py:93
  64.8 5.9 %collective-permute-start = (f32[1,2,13824]{2,1,0:T(2,128)}, f32[1,2,13824]{2,1,0:T(2,128)S(1)}, u32[]{:S(2)}, u32[]{:S(2)}) collective-permute-start(f32[1,2,13824]{2,1,0:T(2,128)} %all-reduce.2.cloned.1.call-done), channel_id=1, source_target_pairs={{0,1},{1,2},{2,3},{3,0},{4,5},{5,6},{6,7},{7,4},{8,9},{9,10},{10,1... | collective-permute-start | bytes 331784 | tf_op jit(solution)/shard_map/ppermute | solution.py:19
  70.6 5.6 %collective-permute-start.1 = (f32[1,2,13824]{2,1,0:T(2,128)S(1)}, f32[1,2,13824]{2,1,0:T(2,128)S(1)}, u32[]{:S(2)}, u32[]{:S(2)}) collective-permute-start(f32[1,2,13824]{2,1,0:T(2,128)S(1)} %collective-permute-done), channel_id=1, source_target_pairs={{0,1},{1,2},{2,3},{3,0},{4,5},{5,6},{6,7},{7,4},{8,9},{9,10},{10,1... | collective-permute-start | bytes 331784 | tf_op jit(solution)/shard_map/ppermute | solution.py:19
  71.3 6.2 %collective-permute-start.2 = (f32[1,2,13824]{2,1,0:T(2,128)}, f32[1,2,13824]{2,1,0:T(2,128)S(1)}, u32[]{:S(2)}, u32[]{:S(2)}) collective-permute-start(f32[1,2,13824]{2,1,0:T(2,128)} %all-reduce.2.cloned.1.call-done), channel_id=1, source_target_pairs={{0,3},{1,0},{2,1},{3,2},{4,7},{5,4},{6,5},{7,6},{8,11},{9,8},{10,9... | collective-permute-start | bytes 331784 | tf_op jit(solution)/shard_map/ppermute | solution.py:21
  78.5 0.9 copy-start
  113.7 3.4 %copy-start.1 = (f32[8,2,13824]{2,1,0:T(2,128)S(1)}, f32[8,2,13824]{2,1,0:T(2,128)}, u32[]{:S(2)}) copy-start(f32[8,2,13824]{2,1,0:T(2,128)} %copy-done) | copy-start | bytes 2654212
Sparse Core Ops, SparseCore 0:
  9.7 55.0 all-reduce.1
